TPU v7x, 1024 devices: a whole 4x8x16 slice. The times are simulated.
1024 devices in a mesh: rep: 64 (over z_lo, x, core), tp: 16 (over y, z_hi).
Axes of the slice: x: 4, y: 8, z: 16 (z_hi: 2, z_lo: 8; z = z_hi * 8 + z_lo), core: 2. Of those that a mesh axis runs over, the one named last changes fastest.
Arguments:
- queries: bfloat16 [64, 4, 16384], P('rep'), may hold values from -18 to 18
- cache_keys: bfloat16 [64, 16, 16, 64, 128], P('rep', 'tp'), may hold values from -8 to 8
- cache_values: bfloat16 [64, 16, 16, 64, 128], P('rep', 'tp'), may hold values from -6 to 6
- page_table: int32 [64, 16, 16], P('rep', 'tp'), may hold values from 0 to 15, each once within a row
- lengths: int32 [64], P('rep'), may hold values from 4 to 2048, as said below
- history: bfloat16 [64, 12, 16384], P('rep', None, 'tp'), may hold values from -10 to 10
- norm_gain: float32 [16384], P('tp'), may hold values from 0.5 to 2
- draft_weight: float32 [16384, 16384], P('tp', 'rep'), may hold values from -0.1640625 to 0.1640625
- targets: int32 [64, 16], replicated, may hold values from 0 to 16383
- accepted: int32 [64], replicated, may hold values from 1 to 16, as said below
Outputs:
- attended: bfloat16 [64, 4, 16384], P('rep', None, 'tp')
- new_weight: float32 [16384, 16384], P('tp', 'rep')
Inputs may be any that keep to these rules, and one draw needn't show every extreme that they name: `lengths`: some replica's sequence has length exactly 2048. `accepted`: some replica trains all 16 rows.
All inputs are finite; a program needn't handle non-finite values.
Results may differ from a plain program's by a relative error of at most 0.01.
Values may be sent and summed in bfloat16 or wider, within the bound.
A program may use at most 32 MiB of HBM per device.

v0:
```python
import jax
import jax.numpy as jnp
from jax import lax
from jax.sharding import PartitionSpec as P

HQ = 128
KVH = 8
HD = 128
D = 16384


learn_rate = 0.5


def partner_2(value, axis, distance):
    mask = 2**distance
    pairs = [(source, source ^ mask) for source in range(lax.axis_size(axis))]
    return lax.ppermute(value, axis, pairs)


def merged(value, axis, join):
    pieces = jax.tree.map(lambda part: lax.all_gather(part, axis), value)
    head = jax.tree.map(lambda part: part[0], pieces)
    tail = jax.tree.map(lambda part: part[1:], pieces)
    so_far, _ = lax.scan(lambda so_far, share: (join(so_far, share), None), head, tail)
    return so_far


def attend(query, keys, values, position, length, kv_local, group_heads):
    steps = query.shape[0]
    limit = length - steps + jnp.arange(steps, dtype=jnp.int32)
    valid = (position[None, :] <= limit[:, None])[:, None, None, :]
    grouped = query.astype(jnp.float32).reshape(steps, kv_local, group_heads, HD)
    scores = jnp.einsum("skgd,pkd->skgp", grouped, keys.astype(jnp.float32)) * HD ** (-0.5)
    top = jnp.max(jnp.where(valid, scores, -1e30), axis=-1)
    expo = jnp.where(valid, jnp.exp(scores - top[..., None]), 0.0)
    total = jnp.sum(expo, axis=-1)
    weighted = jnp.einsum("skgp,pkd->skgd", expo, values.astype(jnp.float32))
    return (top, total, weighted)


def join_softmax(first, second):
    top = jnp.maximum(first[0], second[0])
    left = jnp.exp(first[0] - top)
    right = jnp.exp(second[0] - top)
    return (
        top,
        first[1] * left + second[1] * right,
        first[2] * left[..., None] + second[2] * right[..., None],
    )


def join_stats(first, second):
    top = jnp.maximum(first[0], second[0])
    return (top, first[1] * jnp.exp(first[0] - top) + second[1] * jnp.exp(second[0] - top))


def on_device(
    queries,
    cache_keys,
    cache_values,
    page_table,
    lengths,
    history,
    norm_gain,
    draft_weight,
    targets,
    accepted,
):
    owner = lax.axis_index("tp")
    owners = lax.axis_size("tp")
    kv_local = cache_keys.shape[4] // HD
    sharing = max(1, owners // KVH)
    group_heads = HQ // KVH
    own_heads = HQ // owners
    segment = owner % sharing
    first_head = owner // sharing * kv_local
    table = page_table[0, 0]
    keys = cache_keys[0, 0][table].reshape(-1, kv_local, HD)
    values = cache_values[0, 0][table].reshape(-1, kv_local, HD)
    pages = table.shape[0]
    slots = cache_keys.shape[3]
    position = (
        (jnp.arange(pages, dtype=jnp.int32)[:, None] * sharing + segment) * slots
        + jnp.arange(slots, dtype=jnp.int32)[None, :]
    ).reshape(-1)
    span = kv_local * group_heads * HD
    query = lax.dynamic_slice_in_dim(queries[0], first_head * group_heads * HD, span, 1)
    state = attend(query, keys, values, position, lengths[0], kv_local, group_heads)
    partner = partner_2((state[0], state[1], state[2]), "tp", 0)
    state = join_softmax(state, partner)
    top, total, weighted = state
    steps = query.shape[0]
    heads = (weighted / total[..., None]).reshape(steps, kv_local * group_heads, HD)
    chosen = lax.dynamic_slice_in_dim(heads, segment * own_heads, own_heads, 1)
    attended = chosen.reshape(1, steps, own_heads * HD).astype(jnp.bfloat16)
    raw = jnp.concatenate([attended[0], history[0]], axis=0)
    rows_each = raw.shape[0]
    wide = raw.astype(jnp.float32)
    squares = lax.psum(jnp.sum(wide * wide, axis=-1), "tp")
    row_scale = lax.rsqrt(squares / D + 1e-05)
    scaled_rows = wide * row_scale[:, None] * norm_gain
    gathered = lax.all_gather(scaled_rows, "rep", axis=0, tiled=True)
    partial_value = jnp.dot(
        gathered, draft_weight, precision=lax.Precision.HIGHEST, preferred_element_type=jnp.float32
    )
    logits = lax.psum(partial_value, "tp")
    columns = draft_weight.shape[1]
    column_start = lax.axis_index("rep") * columns
    local_top = jnp.max(logits, axis=-1)
    local_total = jnp.sum(jnp.exp(logits - local_top[:, None]), axis=-1)
    top_all, total_all = merged((local_top, local_total), "rep", join_stats)
    probs = jnp.exp(logits - top_all[:, None]) / total_all[:, None]
    labels = column_start + jnp.arange(columns, dtype=jnp.int32)
    onehot = (targets.reshape(-1)[:, None] == labels[None, :]).astype(jnp.float32)
    keep = (
        (jnp.arange(rows_each, dtype=jnp.int32)[None, :] < accepted[:, None])
        .reshape(-1)
        .astype(jnp.float32)
    )
    delta = (probs - onehot) * keep[:, None]
    grad = jnp.dot(
        gathered.T, delta, precision=lax.Precision.HIGHEST, preferred_element_type=jnp.float32
    )
    return (attended, draft_weight - learn_rate * grad)


def solution(mesh):
    return jax.shard_map(
        on_device,
        mesh=mesh,
        in_specs=(
            P("rep", None, None),
            P("rep", "tp", None, None, None),
            P("rep", "tp", None, None, None),
            P("rep", "tp", None),
            P("rep"),
            P("rep", None, "tp"),
            P("tp"),
            P("tp", "rep"),
            P(),
            P(),
        ),
        out_specs=(P("rep", None, "tp"), P("tp", "rep")),
        check_vma=False,
    )
```

profile of v0, /device:TPU:1, one launch (start us, length us, event | category | flops | bytes accessed | tf_op | source)
XLA Modules:
  0.0 883.9 jit_solution(12709231801653895)
XLA Ops:
  8.0 0.7 fusion.29
  8.7 0.1 add.101
  8.8 0.1 broadcast_compare_fusion
  8.8 0.7 dynamic-slice_bitcast_fusion
  9.6 0.6 gather_fusion.1
  10.2 0.3 select_reduce_fusion
  10.5 0.2 fusion.15
  10.7 19.9 %collective-permute-start.2 = (f32[4,1,16]{2,0,1:T(4,128)S(1)}, f32[4,1,16]{2,0,1:T(4,128)S(1)}, u32[]{:S(2)}, u32[]{:S(2)}) collective-permute-start(f32[4,1,16]{2,0,1:T(4,128)S(1)} %bitcast.78), channel_id=1, source_target_pairs={{0,1},{1,0},{2,3},{3,2},{4,5},{5,4},{6,7},{7,6},{8,9},{9,8},{10,11... | collective-permute-start | bytes 776 | tf_op jit(solution)/shard_map/ppermute | solution.py:18
  30.6 1.9 collective-permute-start
  32.5 1.5 gather_fusion
  34.1 0.2 convolution_bitcast_fusion
  34.3 12.1 %collective-permute-start.1 = (f32[4,1,16,128]{3,2,0,1:T(8,128)S(1)}, f32[4,1,16,128]{3,2,0,1:T(8,128)S(1)}, u32[]{:S(2)}, u32[]{:S(2)}) collective-permute-start(f32[4,1,16,128]{3,2,0,1:T(8,128)S(1)} %convolution_bitcast_fusion), channel_id=1, source_target_pairs={{0,1},{1,0},{2,3},{3,2},{4,5},{5,4},{6,7},{7,6},{8,9},{9,8},{10,11... | collective-permute-start | bytes 98312 | tf_op jit(solution)/shard_map/ppermute | solution.py:18
  46.5 0.1 constant_dynamic-slice_fusion.2
  46.6 2.0 collective-permute-done.1
  48.7 0.1 fusion.26
  48.8 0.9 fusion.19
  49.6 72.0 %psum.14 = f32[16]{0:T(128)S(1)} all-reduce(f32[16]{0:T(128)S(1)} %fusion.19), channel_id=1, replica_groups=mesh['rep'=64,'tp'=16] {'tp'}, use_global_device_ids=true, to_apply=%region_3.4 | all-reduce | flops 16 | bytes 128 | tf_op jit(solution)/shard_map/psum | solution.py:100
  121.6 1.5 fusion.20
  123.2 129.3 %all-gather.4.cloned.1.call-done = f32[1024,1024]{1,0:T(8,128)} async-done(((f32[16,1024]{1,0:T(8,128)}), f32[1024,1024]{1,0:T(8,128)}) %all-gather.4.cloned.1.call-update) | async-done | bytes 4194320 | tf_op jit(solution)/shard_map/all_gather | solution.py:103
  252.5 6.9 fusion.33
  259.4 0.1 copy.13
  259.5 0.1 eq.17
  259.5 0.1 fusion.21
  259.6 0.1 reshape.175
  259.7 0.6 convert_element_type.38
  260.3 356.7 %all-reduce.2.cloned.1.call-done = f32[1024,256]{1,0:T(8,128)} async-done(((f32[1024,256]{1,0:T(8,128)}), f32[1024,256]{1,0:T(8,128)}) %all-reduce.2.cloned.1.call-update) | async-done | bytes 1048592 | tf_op jit(solution)/shard_map/psum | solution.py:107
  617.0 1.5 reduce_max.22
  618.5 129.7 %all-gather = f32[65536]{0:T(1024)S(1)} all-gather(f32[1024]{0:T(1024)S(1)} %reduce_max.22), channel_id=2, replica_groups=mesh['rep'=64,'tp'=16] {'rep'}, dimensions={0}, use_global_device_ids=true | all-gather | bytes 266240 | tf_op jit(solution)/shard_map/all_gather | solution.py:22
  748.2 1.6 exponential_reduce_fusion
  749.8 113.3 %all-gather.1 = f32[65536]{0:T(1024)S(1)} all-gather(f32[1024]{0:T(1024)S(1)} %exponential_reduce_fusion), channel_id=3, replica_groups=mesh['rep'=64,'tp'=16] {'rep'}, dimensions={0}, use_global_device_ids=true | all-gather | bytes 266240 | tf_op jit(solution)/shard_map/all_gather | solution.py:22
  863.3 3.4 while.12
  866.7 10.4 %fusion = f32[1024,256]{1,0:T(8,128)} fusion(f32[1024,256]{1,0:T(8,128)S(1)} %copy-done.2, f32[1024,1024]{1,0:T(8,128)} %all-gather.4.cloned.1.call-done, f32[1024,256]{1,0:T(8,128)S(1)} %copy-done.1, f32[1024]{0:T(1024)S(1)} %reshape.175, s32[256]{0:T(256)S(1)} %iota_add_fusion.1, f32[1024]{0:T(1024)S(1)} %get-tuple-element.31, ...), kind=kOutput, calls=%fused_computation.6 | convolution fusion | flops 3223322624 | bytes 7357440 | tf_op jit(solution)/shard_map/dot_general | solution.py:122
  (157 shorter events, 2.1 us)
Async XLA Ops:
  7.2 2.4 copy-start
  7.2 245.3 %all-gather.4.cloned.1.call-start = ((), (), s32[]{:S(2)}) async-start(), calls=%async_computation | async-start | bytes 4259840 | tf_op jit(solution)/shard_map/all_gather | solution.py:103
  10.7 35.8 %collective-permute-start.2 = (f32[4,1,16]{2,0,1:T(4,128)S(1)}, f32[4,1,16]{2,0,1:T(4,128)S(1)}, u32[]{:S(2)}, u32[]{:S(2)}) collective-permute-start(f32[4,1,16]{2,0,1:T(4,128)S(1)} %bitcast.78), channel_id=1, source_target_pairs={{0,1},{1,0},{2,3},{3,2},{4,5},{5,4},{6,7},{7,6},{8,9},{9,8},{10,11... | collective-permute-start | bytes 776 | tf_op jit(solution)/shard_map/ppermute | solution.py:18
  30.6 15.9 %collective-permute-start = (f32[4,1,16]{2,0,1:T(4,128)S(1)}, f32[4,1,16]{2,0,1:T(4,128)S(1)}, u32[]{:S(2)}, u32[]{:S(2)}) collective-permute-start(f32[4,1,16]{2,0,1:T(4,128)S(1)} %bitcast.77), channel_id=1, source_target_pairs={{0,1},{1,0},{2,3},{3,2},{4,5},{5,4},{6,7},{7,6},{8,9},{9,8},{10,11... | collective-permute-start | bytes 776 | tf_op jit(solution)/shard_map/ppermute | solution.py:18
  34.1 225.3 %copy-start.3 = (s32[64,16]{0,1:T(8,128)S(1)}, s32[64,16]{0,1:T(8,128)}, u32[]{:S(2)}) copy-start(s32[64,16]{0,1:T(8,128)} %param.20) | copy-start | bytes 12292
  34.1 225.4 %copy-start.4 = (s32[64]{0:T(128)S(1)}, s32[64]{0:T(128)}, u32[]{:S(2)}) copy-start(s32[64]{0:T(128)} %param.21) | copy-start | bytes 772
  34.3 14.3 %collective-permute-start.1 = (f32[4,1,16,128]{3,2,0,1:T(8,128)S(1)}, f32[4,1,16,128]{3,2,0,1:T(8,128)S(1)}, u32[]{:S(2)}, u32[]{:S(2)}) collective-permute-start(f32[4,1,16,128]{3,2,0,1:T(8,128)S(1)} %convolution_bitcast_fusion), channel_id=1, source_target_pairs={{0,1},{1,0},{2,3},{3,2},{4,5},{5,4},{6,7},{7,6},{8,9},{9,8},{10,11... | collective-permute-start | bytes 98312 | tf_op jit(solution)/shard_map/ppermute | solution.py:18
  123.1 493.9 %all-reduce.2.cloned.1.call-start = ((), (), s32[]{:S(2)}) async-start(), calls=%async_computation.1 | async-start | bytes 2097152 | tf_op jit(solution)/shard_map/psum | solution.py:107
  259.3 607.3 %copy-start.2 = (f32[1024,256]{1,0:T(8,128)S(1)}, f32[1024,256]{1,0:T(8,128)}, u32[]{:S(2)}) copy-start(f32[1024,256]{1,0:T(8,128)} %param.19) | copy-start | bytes 3145732
  617.0 249.7 %copy-start.1 = (f32[1024,256]{1,0:T(8,128)S(1)}, f32[1024,256]{1,0:T(8,128)}, u32[]{:S(2)}) copy-start(f32[1024,256]{1,0:T(8,128)} %all-reduce.2.cloned.1.call-done) | copy-start | bytes 3145732
Sparse Core Ops, SparseCore 0:
  123.2 129.1 all-gather.3
  259.5 357.4 all-reduce.1
where the time goes:
time: 887 us; the launch traced here: 884 us
  waiting for transfers between devices  488 us (55%)
  blocking collectives  315 us (36%)
  starting transfers between devices  34 us (4%)
  matrix products  17.8 us (2%)
  between operations  15 us (2%)
    psum x1, waiting for transfers between devices, on_device(): logits = lax.psum(partial_value, 'tp')  357 us
    all_gather x2, blocking collectives, merged(): pieces = jax.tree.map(lambda part: lax.all_gather(part, axis), value)  243 us
    all_gather x1, waiting for transfers between devices, on_device(): gathered = lax.all_gather(scaled_rows, 'rep', axis=0, tiled=True)  129 us
    psum x1, blocking collectives, on_device(): squares = lax.psum(jnp.sum(wide * wide, axis=-1), 'tp')  72 us
    ppermute x3, starting transfers between devices, partner_2(): return lax.ppermute(value, axis, pairs)  33.9 us
  transfers between devices with their start and end apart: 5, of which 3 were waited for; matrix products, arithmetic and copies ran while one was open for 0% of the time, Pallas kernels for 0%

commit v1 on v0

v1 whole, which is shorter than its diff:
```python
import jax
import jax.numpy as jnp
from jax import lax
from jax.experimental import pallas as pl
from jax.experimental.pallas import tpu as pltpu
from jax.sharding import PartitionSpec as P

NX, NCORE, NY, NZL = 4, 2, 8, 8
NC = NX * NCORE
FEAT = 1024
COLS = 256
HEADS = 8
STEPS = 4
HD = 128
D = 16384
LEARN_RATE = 0.5
EPS = 1e-5
F32 = jnp.float32
BF16 = jnp.bfloat16
HROWS, AROWS = 96, 32


def remote(src, dst, send, recv, where):
    return pltpu.make_async_remote_copy(
        src_ref=src,
        dst_ref=dst,
        send_sem=send,
        recv_sem=recv,
        device_id=where,
        device_id_type=pl.DeviceIdType.MESH,
    )


def split_bf16(value):
    high = value.astype(BF16)
    return high, (value - high.astype(F32)).astype(BF16)


def dot(a, b):
    return jnp.dot(a, b, preferred_element_type=F32)


def body(
    q_hbm, k_hbm, v_hbm, table, length, hist, gain, w_hbm, targets, accepted,
    att_out, w_out,
    qv, kv, vv, wv, q32, part, px_send, px_recv, blk,
    r8, r4, ra, f4, xh, xa, xt, whi, wlo, gcol, pacc,
    tmp, tk, tcol_h, tcol_a,
    ysh, ysa, yrh, yra, ssh, ssa, srh, sra,
    zsh, zsa, zrh, zra, zssh, zssa, zrsh, zrsa,
    lgh, lga, stzh, stza, stxh, stxa, stch, stca,
    eh, ea, sch, sca, dd,
    load_sem, px_sem, gz_sem, gx_sem, gc_sem, y_sem, z_sem, sz_sem, sx_sem, sc_sem, e_sem, a_sem,
):
    rep = lax.axis_index("rep")
    tp = lax.axis_index("tp")
    core = lax.rem(rep, 2)
    x = lax.rem(rep // 2, NX)
    zl = rep // NC
    zh = lax.rem(tp, 2)
    y = tp // 2
    cc = x * NCORE + core

    def at(zl_=None, x_=None, core_=None, y_=None, zh_=None):
        r = ((zl if zl_ is None else zl_) * NX + (x if x_ is None else x_)) * NCORE + (core if core_ is None else core_)
        t = (y if y_ is None else y_) * 2 + (zh if zh_ is None else zh_)
        return (r, t)

    z_peers = [(j, at(zl_=lax.rem(zl + j, NZL))) for j in range(1, NZL)]
    x_peers = [(j, at(x_=lax.rem(x + j, NX))) for j in range(1, NX)]
    c_peer = at(core_=1 - core)
    y_peers = [(j, lax.rem(y + j, NY)) for j in range(1, NY)]
    h_peer = at(zh_=1 - zh)

    barrier = pltpu.get_barrier_semaphore()
    everyone = [w for _, w in z_peers] + [w for _, w in x_peers] + [c_peer] + [at(y_=t) for _, t in y_peers] + [h_peer]
    for where in everyone:
        pl.semaphore_signal(barrier, inc=1, device_id=where, device_id_type=pl.DeviceIdType.MESH)

    group = tp // 2
    loads = [
        pltpu.make_async_copy(q_hbm.at[0, :, pl.ds(pl.multiple_of(group * 2048, 2048), 2048)], qv, load_sem.at[0]),
        pltpu.make_async_copy(k_hbm, kv, load_sem.at[1]),
        pltpu.make_async_copy(v_hbm, vv, load_sem.at[2]),
        pltpu.make_async_copy(w_hbm, wv, load_sem.at[3]),
    ]
    for load in loads:
        load.start()

    tmp[...] = jnp.zeros_like(tmp)
    part[...] = jnp.zeros_like(part)

    h32 = hist[...].astype(F32)
    r8[cc, zl] = h32[0:8].astype(BF16)
    r4[cc, zl] = h32[8:12].astype(BF16)

    loads[0].wait()
    loads[1].wait()
    loads[2].wait()
    for h in range(16):
        q32[h * STEPS : (h + 1) * STEPS, :] = qv[:, h * HD : (h + 1) * HD].astype(F32)
    scores = lax.dot_general(
        q32[...].astype(BF16), kv[...], (((1,), (1,)), ((), ())), preferred_element_type=F32
    ) * (HD ** -0.5)
    lane = lax.broadcasted_iota(jnp.int32, (64, 1024), 1)
    row = lax.broadcasted_iota(jnp.int32, (64, 1024), 0)
    page = lane // 64
    logical = jnp.zeros((64, 1024), jnp.int32)
    for j in range(16):
        logical = jnp.where(page == table[0, j], j, logical)
    position = (logical * 2 + zh) * 64 + lax.rem(lane, 64)
    valid = position <= length[0] - STEPS + lax.rem(row, STEPS)
    top = jnp.max(jnp.where(valid, scores, -1e30), axis=-1, keepdims=True)
    expo = jnp.where(valid, jnp.exp(scores - top), 0.0)
    total = jnp.sum(expo, axis=-1, keepdims=True)
    e_high, e_low = split_bf16(expo)
    acc = dot(e_high, vv[...]) + dot(e_low, vv[...])
    part[0:64, :] = acc
    tmp[0:64, :] = jnp.broadcast_to(top, (64, 128))
    tmp[64:128, :] = jnp.broadcast_to(total, (64, 128))
    stat_rows = jnp.transpose(tmp[...])
    other = pl.multiple_of((1 - zh) * 32, 32)
    px_send[0:32, :] = part[pl.ds(other, 32), :]
    px_send[32:40, :] = stat_rows[0:8, :]

    pl.semaphore_wait(barrier, len(everyone))
    px = remote(px_send, px_recv, px_sem.at[0], px_sem.at[1], h_peer)
    px.start()

    def gather(buf, i):
        z = [
            remote(buf.at[cc, zl], buf.at[cc, zl], gz_sem.at[i, 0, j], gz_sem.at[i, 1, j], where)
            for j, where in z_peers
        ]
        xs = [
            remote(buf.at[cc], buf.at[cc], gx_sem.at[i, 0, j], gx_sem.at[i, 1, j], where)
            for j, where in x_peers
        ]
        cs = []
        for j in range(NX):
            k = lax.rem(x + j, NX) * NCORE + core
            cs.append(remote(buf.at[k], buf.at[k], gc_sem.at[i, 0, j], gc_sem.at[i, 1, j], c_peer))
        return z, xs, cs

    def start(copies):
        for copy in copies:
            copy.start()

    def wait(copies):
        for copy in copies:
            copy.wait()

    g8, g4, ga = gather(r8, 0), gather(r4, 1), gather(ra, 2)
    start(g8[0] + g4[0])

    loads[3].wait()

    def make_w(b, _):
        rows = pl.ds(pl.multiple_of(b * 128, 128), 128)
        g = jnp.transpose(jnp.broadcast_to(gain[0:1, rows], (128, 128)))
        gcol[rows, :] = g
        w = wv[rows, :] * jnp.concatenate([g, g], axis=1)
        high, low = split_bf16(w)
        whi[rows, :] = high
        wlo[rows, :] = low
        return 0

    lax.fori_loop(0, 8, make_w, 0)

    acc_row = accepted[...].astype(F32)
    ri = lax.broadcasted_iota(jnp.int32, (64, 64), 0)
    li = lax.broadcasted_iota(jnp.int32, (64, 64), 1)
    acc_col = jnp.sum(jnp.where(ri == li, jnp.broadcast_to(acc_row, (64, 64)), 0.0), axis=1, keepdims=True)
    ii = lax.broadcasted_iota(jnp.int32, (64, 16), 1).astype(F32)
    tk[...] = jnp.where(ii < acc_col, targets[...].astype(F32), -1.0)

    def target_cols(n, zl_of, i_of, out):
        rho = lax.broadcasted_iota(jnp.int32, (n, 64), 0)
        rep_lane = lax.broadcasted_iota(jnp.int32, (n, 64), 1)
        rho16 = lax.broadcasted_iota(jnp.int32, (n, 16), 0)
        lane16 = lax.broadcasted_iota(jnp.int32, (n, 16), 1)

        def one(c, _):
            pick = (rep_lane == zl_of(rho) * NC + c).astype(F32)
            rows = jnp.dot(pick, tk[...], precision=lax.Precision.HIGHEST, preferred_element_type=F32)
            col = jnp.sum(jnp.where(lane16 == i_of(rho16), rows, 0.0), axis=1, keepdims=True)
            out[c] = jnp.broadcast_to(col, (n, 128))
            return 0

        lax.fori_loop(0, NY, one, 0)

    target_cols(
        HROWS,
        lambda p: jnp.where(p < 64, p // 8, (p - 64) // 4),
        lambda p: jnp.where(p < 64, 4 + lax.rem(p, 8), 12 + lax.rem(p, 4)),
        tcol_h,
    )
    target_cols(AROWS, lambda p: p // 4, lambda p: lax.rem(p, 4), tcol_a)

    wait(g8[0] + g4[0])
    start(g8[1] + g4[1])

    px.wait()
    tmp[0:64, :] = jnp.broadcast_to(stat_rows[0:1, :], (64, 128))
    tmp[64:128, :] = jnp.broadcast_to(px_recv[32:33, :], (64, 128))
    tmp[...] = jnp.transpose(tmp[...])
    mine = pl.multiple_of(zh * 32, 32)
    top_a = tmp[pl.ds(mine, 32), 0:1]
    sum_a = tmp[pl.ds(mine + 64, 32), 0:1]
    top_b = tmp[pl.ds(mine, 32), 64:65]
    sum_b = tmp[pl.ds(mine + 64, 32), 64:65]
    top_ab = jnp.maximum(top_a, top_b)
    left = jnp.exp(top_a - top_ab)
    right = jnp.exp(top_b - top_ab)
    joined = (part[pl.ds(mine, 32), :] * left + px_recv[0:32, :] * right) / (sum_a * left + sum_b * right)
    part[0:32, :] = joined
    for h in range(HEADS):
        blk[:, h * HD : (h + 1) * HD] = part[h * STEPS : (h + 1) * STEPS, :]
    own = blk[...].astype(BF16)
    ra[cc, zl] = own
    att_out[0] = own
    start(ga[0])

    wait(g8[1] + g4[1])
    start(g8[2] + g4[2])
    wait(ga[0])
    start(ga[1])

    def row_form(col, n):
        tmp[0:n, :] = jnp.broadcast_to(col, (n, 128))
        return jnp.transpose(tmp[...])[0:8, :]

    wait(g8[2] + g4[2])

    def prep_h(c, _):
        v8 = r8[c].astype(F32).reshape(64, FEAT)
        base = pl.multiple_of(c * HROWS, 32)
        for j in range(4):
            f4[j, 0:4, :] = r4[c, 2 * j].astype(F32)
            f4[j, 4:8, :] = r4[c, 2 * j + 1].astype(F32)
        v4 = f4[...].reshape(32, FEAT)
        xh[pl.ds(base, 64), :] = v8.astype(BF16)
        xh[pl.ds(pl.multiple_of(base + 64, 32), 32), :] = v4.astype(BF16)
        tmp[0:64, :] = jnp.broadcast_to(jnp.sum(v8 * v8, axis=1, keepdims=True), (64, 128))
        tmp[64:96, :] = jnp.broadcast_to(jnp.sum(v4 * v4, axis=1, keepdims=True), (32, 128))
        ssh[c] = jnp.transpose(tmp[...])[0:8, :]
        return 0

    lax.fori_loop(0, NY, prep_h, 0)
    pacc[...] = dot(xh[...], whi[...]) + dot(xh[...], wlo[...])

    def pack_h(c, _):
        ysh[c] = pacc[pl.ds(pl.multiple_of(c * HROWS, 32), HROWS), :].astype(BF16)
        return 0

    lax.fori_loop(0, NY, pack_h, 0)

    def scatter(i, send, ss_send, recv, ss_recv):
        copies = []
        for j, t in y_peers:
            where = at(y_=t)
            copies.append(remote(ss_send.at[t], ss_recv.at[y], y_sem.at[i, 0, j], y_sem.at[i, 1, j], where))
            copies.append(remote(send.at[t], recv.at[y], y_sem.at[i, 2, j], y_sem.at[i, 3, j], where))
        return copies

    rs_h = scatter(0, ysh, ssh, yrh, srh)
    rs_a = scatter(1, ysa, ssa, yra, sra)
    start(rs_h)

    wait(ga[1])
    start(ga[2])

    def transpose_x(src, off, count):
        def one(b, _):
            rows = pl.ds(pl.multiple_of(b * 128, 128), 128)
            lanes = pl.ds(pl.multiple_of(off + b * 128, 128), 128)
            xt[:, lanes] = jnp.transpose(src[rows, :].astype(F32)).astype(BF16)
            return 0

        lax.fori_loop(0, count, one, 0)

    wait(ga[2])

    def prep_a(c, _):
        for j in range(4):
            f4[j, 0:4, :] = ra[c, 2 * j].astype(F32)
            f4[j, 4:8, :] = ra[c, 2 * j + 1].astype(F32)
        v4 = f4[...].reshape(32, FEAT)
        xa[pl.ds(pl.multiple_of(c * AROWS, 32), 32), :] = v4.astype(BF16)
        ssa[c] = row_form(jnp.sum(v4 * v4, axis=1, keepdims=True), AROWS)
        return 0

    lax.fori_loop(0, NY, prep_a, 0)
    pacc[0:256, :] = dot(xa[...], whi[...]) + dot(xa[...], wlo[...])

    def pack_a(c, _):
        ysa[c] = pacc[pl.ds(pl.multiple_of(c * AROWS, 32), AROWS), :].astype(BF16)
        return 0

    lax.fori_loop(0, NY, pack_a, 0)
    start(rs_a)
    transpose_x(xh, 0, 6)
    transpose_x(xa, 768, 2)

    def exchange(i, zs, zss, zr, zrs):
        return [
            remote(zss, zrs, z_sem.at[i, 0], z_sem.at[i, 1], h_peer),
            remote(zs, zr, z_sem.at[i, 2], z_sem.at[i, 3], h_peer),
        ]

    zx_h = exchange(0, zsh, zssh, zrh, zrsh)
    zx_a = exchange(1, zsa, zssa, zra, zrsa)

    def sum_y(copies, send, ss_send, recv, ss_recv, zs, zss, lg, zx):
        wait(copies)
        lg[...] = send[y].astype(F32)
        total = ss_send[y]
        for j in range(1, NY):
            t = lax.rem(y + j, NY)
            lg[...] += recv[t].astype(F32)
            total = total + ss_recv[t]
        zs[...] = lg[...].astype(BF16)
        zss[...] = total
        start(zx)

    sum_y(rs_h, ysh, ssh, yrh, srh, zsh, zssh, lgh, zx_h)
    sum_y(rs_a, ysa, ssa, yra, sra, zsa, zssa, lga, zx_a)

    def column(row_ref_value, n):
        return jnp.transpose(jnp.broadcast_to(row_ref_value, (128, 128)))[0:n, :]

    def gather_y(i, buf, sem):
        return [
            remote(buf.at[y], buf.at[y], sem.at[i, 0, j], sem.at[i, 1, j], at(y_=t)) for j, t in y_peers
        ]

    def stats_copies(i, stz, stx, stc):
        z = [remote(stz.at[zl], stz.at[zl], sz_sem.at[i, 0, j], sz_sem.at[i, 1, j], w) for j, w in z_peers]
        xs = [remote(stx.at[x], stx.at[x], sx_sem.at[i, 0, j], sx_sem.at[i, 1, j], w) for j, w in x_peers]
        c = [remote(stc.at[core], stc.at[core], sc_sem.at[i, 0], sc_sem.at[i, 1], c_peer)]
        return z, xs, c

    st_h = stats_copies(0, stzh, stxh, stch)
    st_a = stats_copies(1, stza, stxa, stca)
    e_h, e_a = gather_y(0, eh, e_sem), gather_y(1, ea, e_sem)
    s_h, s_a = gather_y(0, sch, a_sem), gather_y(1, sca, a_sem)

    def logits(n, zx, zr, zrs, zss, lg, stz, st, e_buf, e_copies):
        wait(zx)
        ss = zss[...] + zrs[...]
        scale_row = lax.rsqrt(ss / D + EPS)
        scale = column(scale_row[0:1, :], n)
        value = (lg[...] + zr[...].astype(F32)) * jnp.concatenate([scale, scale], axis=1)
        top_l = jnp.max(value, axis=1, keepdims=True)
        ex = jnp.exp(value - top_l)
        sum_l = jnp.sum(ex, axis=1, keepdims=True)
        e_buf[y] = ex.astype(BF16)
        m_row = row_form(top_l, n)
        l_row = row_form(sum_l, n)
        stz[zl, 0:4, :] = m_row[0:4, :]
        stz[zl, 4:8, :] = l_row[0:4, :]
        start(st[0])
        start(e_copies)
        return scale_row, m_row

    def join(buf, n):
        m = buf[0, 0:4, :]
        for j in range(1, n):
            m = jnp.maximum(m, buf[j, 0:4, :])
        total = buf[0, 4:8, :] * jnp.exp(buf[0, 0:4, :] - m)
        for j in range(1, n):
            total = total + buf[j, 4:8, :] * jnp.exp(buf[j, 0:4, :] - m)
        return m, total

    def pass_on(copies, buf, n, out, slot, nxt):
        wait(copies)
        m, total = join(buf, n)
        out[slot, 0:4, :] = m
        out[slot, 4:8, :] = total
        start(nxt)

    def finish(copies, stc, sc, scale_row, m_row, nxt):
        wait(copies)
        m, total = join(stc, 2)
        sc[y, 0:4, :] = jnp.exp(m_row[0:4, :] - m) / total
        sc[y, 4:8, :] = scale_row[0:4, :]
        start(nxt)

    row_h = logits(HROWS, zx_h, zrh, zrsh, zssh, lgh, stzh, st_h, eh, e_h)
    row_a = logits(AROWS, zx_a, zra, zrsa, zssa, lga, stza, st_a, ea, e_a)
    pass_on(st_h[0], stzh, NZL, stxh, x, st_h[1])
    pass_on(st_a[0], stza, NZL, stxa, x, st_a[1])
    pass_on(st_h[1], stxh, NX, stch, core, st_h[2])
    pass_on(st_a[1], stxa, NX, stca, core, st_a[2])
    finish(st_h[2], stch, sch, row_h[0], row_h[1], s_h)
    finish(st_a[2], stca, sca, row_a[0], row_a[1], s_a)

    labels = (lax.broadcasted_iota(jnp.int32, (1, COLS), 1) + rep * COLS).astype(F32)

    def deltas(n, off, e_buf, sc, tcol):
        def one(c, _):
            s = column(sc[c, 0:1, :], n)
            scale = column(sc[c, 4:5, :], n)
            t = tcol[c]
            t2 = jnp.concatenate([t, t], axis=1)
            p = e_buf[c].astype(F32) * jnp.concatenate([s, s], axis=1)
            delta = jnp.where(t2 >= 0.0, p - jnp.where(t2 == labels, 1.0, 0.0), 0.0)
            delta = delta * jnp.concatenate([scale, scale], axis=1)
            dd[pl.ds(pl.multiple_of(off + c * n, 32), n), :] = delta.astype(BF16)
            return 0

        lax.fori_loop(0, NY, one, 0)

    wait(e_h)
    wait(s_h)
    deltas(HROWS, 0, eh, sch, tcol_h)
    wait(e_a)
    wait(s_a)
    deltas(AROWS, 768, ea, sca, tcol_a)

    def update(b, _):
        rows = pl.ds(pl.multiple_of(b * 256, 256), 256)
        grad = dot(xt[rows, :], dd[...])
        g = gcol[rows, :] * LEARN_RATE
        w_out[rows, :] = wv[rows, :] - jnp.concatenate([g, g], axis=1) * grad
        return 0

    lax.fori_loop(0, 4, update, 0)


def on_device(queries, cache_keys, cache_values, page_table, lengths, history, norm_gain, draft_weight, targets, accepted):
    vmem = pl.BlockSpec(memory_space=pltpu.VMEM)
    smem = pl.BlockSpec(memory_space=pltpu.SMEM)
    hbm = pl.BlockSpec(memory_space=pl.ANY)
    V = pltpu.VMEM
    dma = pltpu.SemaphoreType.DMA
    attended, new_weight = pl.pallas_call(
        body,
        out_shape=(
            jax.ShapeDtypeStruct((1, STEPS, FEAT), BF16),
            jax.ShapeDtypeStruct((FEAT, COLS), F32),
        ),
        in_specs=[hbm, hbm, hbm, smem, smem, vmem, vmem, hbm, vmem, vmem],
        out_specs=(vmem, vmem),
        scratch_shapes=[
            V((STEPS, 2048), BF16), V((1024, HD), BF16), V((1024, HD), BF16), V((FEAT, COLS), F32),
            V((64, HD), F32), V((64, HD), F32), V((40, HD), F32), V((40, HD), F32), V((STEPS, FEAT), F32),
            V((NC, NZL, 8, FEAT), BF16), V((NC, NZL, 4, FEAT), BF16), V((NC, NZL, 4, FEAT), BF16),
            V((4, 8, FEAT), F32), V((768, FEAT), BF16), V((256, FEAT), BF16), V((FEAT, 1024), BF16),
            V((FEAT, COLS), BF16), V((FEAT, COLS), BF16), V((FEAT, 128), F32), V((768, COLS), F32),
            V((128, 128), F32), V((64, 16), F32), V((NY, HROWS, 128), F32), V((NY, AROWS, 128), F32),
            V((NY, HROWS, COLS), BF16), V((NY, AROWS, COLS), BF16), V((NY, HROWS, COLS), BF16), V((NY, AROWS, COLS), BF16),
            V((NY, 8, 128), F32), V((NY, 8, 128), F32), V((NY, 8, 128), F32), V((NY, 8, 128), F32),
            V((HROWS, COLS), BF16), V((AROWS, COLS), BF16), V((HROWS, COLS), BF16), V((AROWS, COLS), BF16),
            V((8, 128), F32), V((8, 128), F32), V((8, 128), F32), V((8, 128), F32),
            V((HROWS, COLS), F32), V((AROWS, COLS), F32),
            V((NZL, 8, 128), F32), V((NZL, 8, 128), F32), V((NX, 8, 128), F32), V((NX, 8, 128), F32),
            V((2, 8, 128), F32), V((2, 8, 128), F32),
            V((NY, HROWS, COLS), BF16), V((NY, AROWS, COLS), BF16), V((NY, 8, 128), F32), V((NY, 8, 128), F32),
            V((1024, COLS), BF16),
            dma((4,)), dma((2,)), dma((3, 2, 8)), dma((3, 2, 4)), dma((3, 2, 4)), dma((2, 4, 8)), dma((2, 4)),
            dma((2, 2, 8)), dma((2, 2, 4)), dma((2, 2)), dma((2, 2, 8)), dma((2, 2, 8)),
        ],
        compiler_params=pltpu.CompilerParams(collective_id=0, has_side_effects=True, vmem_limit_bytes=48 * 1024 * 1024),
        name="decode_draft_step",
    )(
        queries,
        cache_keys.reshape(1024, HD),
        cache_values.reshape(1024, HD),
        page_table.reshape(1, 16),
        lengths,
        history.reshape(12, FEAT),
        norm_gain.reshape(1, FEAT),
        draft_weight,
        targets,
        accepted.reshape(1, 64),
    )
    return attended, new_weight


def solution(mesh):
    return jax.shard_map(
        on_device,
        mesh=mesh,
        in_specs=(
            P("rep", None, None),
            P("rep", "tp", None, None, None),
            P("rep", "tp", None, None, None),
            P("rep", "tp", None),
            P("rep"),
            P("rep", None, "tp"),
            P("tp"),
            P("tp", "rep"),
            P(),
            P(),
        ),
        out_specs=(P("rep", None, "tp"), P("tp", "rep")),
        check_vma=False,
    )
```

time: 887 us -> 105 us (0.12)
  waiting for transfers between devices: 488 us -> 0 us
  blocking collectives: 315 us -> 0 us
  Pallas kernels: 0 us -> 97.3 us
  starting transfers between devices: 34 us -> 0 us
  matrix products: 17.8 us -> 0 us
  between operations: 15 us -> 1.33 us
    psum x1 -> x0, waiting for transfers between devices: 357 us -> none  [on_device(): logits = lax.psum(partial_value, 'tp')]
    all_gather x2 -> x0, blocking collectives: 243 us -> none  [merged(): pieces = jax.tree.map(lambda part: lax.all_gather(part, axis), value)]
    all_gather x1 -> x0, waiting for transfers between devices: 129 us -> none  [on_device(): gathered = lax.all_gather(scaled_rows, 'rep', axis=0, tiled=True)]
    pallas_call x0 -> x1, Pallas kernels: none -> 97.3 us  [on_device(): pl.pallas_call(body, out_shape=(jax.ShapeDtypeStruct((1, STEPS, FEAT), BF...]
    psum x1 -> x0, blocking collectives: 72 us -> none  [on_device(): squares = lax.psum(jnp.sum(wide * wide, axis=-1), 'tp')]
    ppermute x3 -> x0, starting transfers between devices: 33.9 us -> none  [partner_2(): return lax.ppermute(value, axis, pairs)]
    dot_general x4 -> x0, matrix products: 17.8 us -> none  [the longest x1 10.4 us: on_device(): jnp.dot(gathered.T, delta, precision=lax.Precision.HIGHEST, preferred_ele...]
  transfers between devices with their start and end apart: 5 -> 0, of which waited for: 3 -> 0; matrix products, arithmetic and copies ran while one was open for 0% -> 0% of each run, Pallas kernels for 0% -> 0%
where the time goes in v1:
time: 105 us
  Pallas kernels  97.3 us (93%)
  local copies, waits for them, and re-layouts  6.31 us (6%)
  between operations  1.33 us (1%)
    pallas_call x1, Pallas kernels, on_device(): pl.pallas_call(body, out_shape=(jax.ShapeDtypeStruct((1, STEPS, FEAT), BF...  97.3 us
    unnamed x21, local copies, waits for them, and re-layouts  6.31 us

profile of v1, /device:TPU:1, one launch (start us, length us, event | category | flops | bytes accessed | tf_op | source)
XLA Modules:
  0.0 105.0 jit_solution(12524877271756973712)
XLA Ops:
  0.6 0.0 copy-start.8
  0.6 0.0 copy-start.4
  1.3 0.0 copy-done.8
  1.3 0.0 copy-start.5
  1.3 0.0 copy-start.6
  1.3 0.0 copy-start.7
  1.3 0.1 copy.12.targets
  1.4 0.0 copy-done.4
  1.4 0.6 copy-done.5
  2.0 0.0 copy-done.6
  2.0 0.0 copy-done.7
  2.0 0.0 copy-start
  2.0 1.2 %copy-done = f32[1024,256]{1,0:T(8,128)S(1)} copy-done((f32[1024,256]{1,0:T(8,128)S(1)}, f32[1024,256]{1,0:T(8,128)}, u32[]{:S(2)}) %copy-start) | copy-done | bytes 1048600
  3.3 0.0 copy-start.1
  3.3 0.9 copy-done.1
  4.2 0.0 copy-start.2
  4.2 0.9 copy-done.2
  5.2 0.0 copy-start.3
  5.2 0.9 copy-done.3
  6.1 97.3 %decode_draft_step.1 = (bf16[1,4,1024]{2,1,0:T(4,128)(2,1)S(1)}, f32[1024,256]{1,0:T(8,128)S(1)}) custom-call(bf16[1,4,16384]{2,1,0:T(4,128)(2,1)S(1)} %copy-done.3, bf16[1024,128]{1,0:T(8,128)(2,1)S(1)} %bitcast.6, bf16[1024,128]{1,0:T(8,128)(2,1)S(1)} %bitcast.7, s32[1,16]{1,0:T(1,128)S(1)} %bitcast.10, s32[1]{0:T(128)S(6)} %copy.15.length, ...), custom_call_target="tpu_custom_call" | custom-call | tf_op jit(solution)/shard_map/decode_draft_step/pallas_call | solution.py:437
  103.4 0.6 copy.16
  104.0 1.0 copy.17
Async XLA Ops:
  0.6 0.7 copy-start.8
  0.6 0.8 copy-start.4
  1.3 0.7 copy-start.5
  1.3 0.7 copy-start.6
  1.3 0.7 copy-start.7
  2.0 1.2 %copy-start = (f32[1024,256]{1,0:T(8,128)S(1)}, f32[1024,256]{1,0:T(8,128)}, u32[]{:S(2)}) copy-start(f32[1024,256]{1,0:T(8,128)} %w_hbm.1) | copy-start | bytes 3145732
  3.3 0.9 copy-start.1
  4.2 0.9 copy-start.2
  5.2 0.9 copy-start.3

commit v2 on v1

v2 whole, which is shorter than its diff:
```python
import jax
import jax.numpy as jnp
from jax import lax
from jax.experimental import pallas as pl
from jax.experimental.pallas import tpu as pltpu
from jax.sharding import PartitionSpec as P

NX, NCORE, NY, NZL = 4, 2, 8, 8
NC = NX * NCORE
FEAT = 1024
COLS = 256
HEADS = 8
STEPS = 4
HD = 128
D = 16384
LEARN_RATE = 0.5
EPS = 1e-5
F32 = jnp.float32
BF16 = jnp.bfloat16
HROWS, AROWS = 96, 32


def remote(src, dst, send, recv, where):
    return pltpu.make_async_remote_copy(
        src_ref=src,
        dst_ref=dst,
        send_sem=send,
        recv_sem=recv,
        device_id=where,
        device_id_type=pl.DeviceIdType.MESH,
    )


def split_bf16(value):
    high = value.astype(BF16)
    return high, (value - high.astype(F32)).astype(BF16)


def dot(a, b):
    return jnp.dot(a, b, preferred_element_type=F32)


def body(
    q_hbm, k_hbm, v_hbm, table_hbm, length, hist_hbm, gain_hbm, w_hbm, targets_hbm, accepted_hbm,
    att_out, w_out,
    table, hist, gain, targets, accepted,
    qv, kv, vv, wv, q32, part, px_send, px_recv, blk,
    r8, r4, ra, f4, xr, xt, whi, wlo, gcol, pacc,
    tmp, tmp2, tk, tcol,
    ysh, ysa, yrh, yra, ssh, ssa, srh, sra,
    zsh, zsa, zrh, zra, zssh, zssa, zrsh, zrsa,
    lg, stz, stp, stc, eb, sc, dd,
    load_sem, px_sem, gz_sem, gx_sem, gc_sem, y_sem, z_sem, sz_sem, sp_sem, sc_sem, e_sem, a_sem,
):
    rep = lax.axis_index("rep")
    tp = lax.axis_index("tp")
    core = lax.rem(rep, 2)
    x = lax.rem(rep // 2, NX)
    zl = rep // NC
    zh = lax.rem(tp, 2)
    y = tp // 2
    cc = x * NCORE + core

    def at(zl_=None, x_=None, core_=None, y_=None, zh_=None):
        r = ((zl if zl_ is None else zl_) * NX + (x if x_ is None else x_)) * NCORE + (core if core_ is None else core_)
        t = (y if y_ is None else y_) * 2 + (zh if zh_ is None else zh_)
        return (r, t)

    half = zl // 4
    near = [half * 4 + lax.rem(lax.rem(zl, 4) + j, 4) for j in range(1, 4)]
    far = [(1 - half) * 4 + lax.rem(lax.rem(zl, 4) + j, 4) for j in range(4)]
    z_peers = [(j, at(zl_=t)) for j, t in enumerate(near + far)]
    x_peers = [(j, at(x_=lax.rem(x + j, NX))) for j in range(1, NX)]
    plane = [
        (i, j, at(x_=lax.rem(x + i, NX), y_=lax.rem(y + j, NY)))
        for i in range(NX)
        for j in range(NY)
        if i or j
    ]
    c_peer = at(core_=1 - core)
    y_peers = [(j, lax.rem(y + j, NY)) for j in range(1, NY)]
    h_peer = at(zh_=1 - zh)

    barrier = pltpu.get_barrier_semaphore()
    everyone = [h_peer] + [w for _, w in z_peers] + [w for _, _, w in plane] + [c_peer]
    for where in everyone:
        pl.semaphore_signal(barrier, inc=1, device_id=where, device_id_type=pl.DeviceIdType.MESH)

    group = tp // 2
    loads = [
        pltpu.make_async_copy(src, dst, load_sem.at[i])
        for i, (src, dst) in enumerate(
            [
                (q_hbm.at[0, :, pl.ds(pl.multiple_of(group * 2048, 2048), 2048)], qv),
                (k_hbm, kv),
                (table_hbm, table),
                (v_hbm, vv),
                (hist_hbm, hist),
                (gain_hbm, gain),
                (w_hbm, wv),
                (targets_hbm, targets),
                (accepted_hbm, accepted),
            ]
        )
    ]
    for load in loads:
        load.start()

    def start(copies):
        for copy in copies:
            copy.start()

    def wait(copies):
        for copy in copies:
            copy.wait()

    tmp[...] = jnp.zeros_like(tmp)
    tmp2[...] = jnp.zeros_like(tmp2)

    wait(loads[0:3])
    lane = lax.broadcasted_iota(jnp.int32, (8, 1024), 1)
    page = lane // 64
    logical = jnp.zeros((8, 1024), jnp.int32)
    for j in range(16):
        logical = jnp.where(page == table[0, j], j, logical)
    position = (logical * 2 + zh) * 64 + lax.rem(lane, 64)
    row = lax.broadcasted_iota(jnp.int32, (8, 1024), 0)
    valid8 = position <= length[0] - STEPS + lax.rem(row, STEPS)
    bias = jnp.where(valid8, 0.0, -1e30)
    for h in range(16):
        q32[h * STEPS : (h + 1) * STEPS, :] = qv[:, h * HD : (h + 1) * HD].astype(F32)
    scores = lax.dot_general(
        q32[...].astype(BF16), kv[...], (((1,), (1,)), ((), ())), preferred_element_type=F32
    ) * (HD ** -0.5)
    valid = jnp.concatenate([bias] * 8, axis=0) == 0.0
    top = jnp.max(jnp.where(valid, scores, -1e30), axis=-1, keepdims=True)
    expo = jnp.where(valid, jnp.exp(scores - top), 0.0)
    total = jnp.sum(expo, axis=-1, keepdims=True)
    e_high, e_low = split_bf16(expo)
    tmp[0:64, :] = jnp.broadcast_to(top, (64, 128))
    tmp[64:128, :] = jnp.broadcast_to(total, (64, 128))
    stat_rows = jnp.transpose(tmp[...])
    loads[3].wait()
    part[...] = dot(e_high, vv[...]) + dot(e_low, vv[...])
    other = pl.multiple_of((1 - zh) * 32, 32)
    px_send[0:32, :] = part[pl.ds(other, 32), :]
    px_send[32:40, :] = stat_rows[0:8, :]

    loads[4].wait()
    h32 = hist[...].astype(F32)
    r8[cc, zl] = h32[0:8].astype(BF16)
    r4[cc, zl] = h32[8:12].astype(BF16)

    pl.semaphore_wait(barrier, len(everyone))
    px = remote(px_send, px_recv, px_sem.at[0], px_sem.at[1], h_peer)
    px.start()

    def gather(buf, i):
        z = [
            remote(buf.at[cc, zl], buf.at[cc, zl], gz_sem.at[i, 0, j], gz_sem.at[i, 1, j], where)
            for j, where in z_peers
        ]

        def piece(k, h):
            return buf.at[k, pl.ds(h * 4, 4)]

        xs, cs = [], []
        for slot, h in ((0, half), (1, 1 - half)):
            xs.append(
                [
                    remote(piece(cc, h), piece(cc, h), gx_sem.at[i, slot, 0, j], gx_sem.at[i, slot, 1, j], where)
                    for j, where in x_peers
                ]
            )
            one = []
            for j in range(NX):
                k = lax.rem(x + j, NX) * NCORE + core
                one.append(remote(piece(k, h), piece(k, h), gc_sem.at[i, slot, 0, j], gc_sem.at[i, slot, 1, j], c_peer))
            cs.append(one)
        return z[0:3], z[3:7], xs, cs

    g8, g4, ga = gather(r8, 0), gather(r4, 1), gather(ra, 2)
    start(g8[0] + g4[0] + g8[1] + g4[1])

    wait(loads[5:7])

    def make_w(b, _):
        rows = pl.ds(pl.multiple_of(b * 128, 128), 128)
        g = jnp.transpose(jnp.broadcast_to(gain[0:1, rows], (128, 128)))
        gcol[rows, :] = g
        w = wv[rows, :] * jnp.concatenate([g, g], axis=1)
        high, low = split_bf16(w)
        whi[rows, :] = high
        wlo[rows, :] = low
        return 0

    lax.fori_loop(0, 8, make_w, 0)

    wait(g8[0] + g4[0])
    start(g8[2][0] + g4[2][0])

    tmp[0:64, :] = jnp.broadcast_to(stat_rows[0:1, :], (64, 128))
    px.wait()
    tmp[64:128, :] = jnp.broadcast_to(px_recv[32:33, :], (64, 128))
    tmp[...] = jnp.transpose(tmp[...])
    mine = pl.multiple_of(zh * 32, 32)
    top_a = tmp[pl.ds(mine, 32), 0:1]
    sum_a = tmp[pl.ds(mine + 64, 32), 0:1]
    top_b = tmp[pl.ds(mine, 32), 64:65]
    sum_b = tmp[pl.ds(mine + 64, 32), 64:65]
    top_ab = jnp.maximum(top_a, top_b)
    left = jnp.exp(top_a - top_ab)
    right = jnp.exp(top_b - top_ab)
    joined = (part[pl.ds(mine, 32), :] * left + px_recv[0:32, :] * right) / (sum_a * left + sum_b * right)
    part[0:32, :] = joined
    for h in range(HEADS):
        blk[:, h * HD : (h + 1) * HD] = part[h * STEPS : (h + 1) * STEPS, :]
    own = blk[...].astype(BF16)
    ra[cc, zl] = own
    start(ga[0] + ga[1])
    att_out[0] = own

    wait(g8[1] + g4[1])
    start(g8[2][1] + g4[2][1])

    wait(loads[7:9])
    ii = lax.broadcasted_iota(jnp.int32, (16, 64), 0)
    tk[...] = jnp.where(ii < accepted[...], targets[...], -1).astype(F32)
    rho = lax.broadcasted_iota(jnp.int32, (128, 64), 0)
    rep_lane = lax.broadcasted_iota(jnp.int32, (128, 64), 1)
    zl_of = jnp.where(rho < 64, rho // 8, jnp.where(rho < 96, (rho - 64) // 4, (rho - 96) // 4))
    rho16 = lax.broadcasted_iota(jnp.int32, (128, 16), 0)
    lane16 = lax.broadcasted_iota(jnp.int32, (128, 16), 1)
    i_of = jnp.where(rho16 < 64, 4 + lax.rem(rho16, 8), jnp.where(rho16 < 96, 12, 0) + lax.rem(rho16, 4))

    def target_cols(c, _):
        pick = (rep_lane == zl_of * NC + c).astype(F32)
        rows = lax.dot_general(
            pick, tk[...], (((1,), (1,)), ((), ())), precision=lax.Precision.HIGHEST, preferred_element_type=F32
        )
        col = jnp.sum(jnp.where(lane16 == i_of, rows, 0.0), axis=1, keepdims=True)
        tcol[c] = jnp.broadcast_to(col, (128, 128))
        return 0

    lax.fori_loop(0, NY, target_cols, 0)

    wait(g8[2][0] + g4[2][0])
    start(g8[3][0] + g4[3][0])
    wait(g8[2][1] + g4[2][1])
    start(g8[3][1] + g4[3][1])

    def narrow_rows(buf, c):
        for j in range(4):
            f4[j, 0:4, :] = buf[c, 2 * j].astype(F32)
            f4[j, 4:8, :] = buf[c, 2 * j + 1].astype(F32)
        return f4[...].reshape(32, FEAT)

    wait(g8[3][0] + g4[3][0] + g8[3][1] + g4[3][1])

    def prep_h(c, _):
        v8 = r8[c].astype(F32).reshape(64, FEAT)
        v4 = narrow_rows(r4, c)
        xr[c, 0:64, :] = v8.astype(BF16)
        xr[c, 64:96, :] = v4.astype(BF16)
        tmp[0:64, :] = jnp.broadcast_to(jnp.sum(v8 * v8, axis=1, keepdims=True), (64, 128))
        tmp[64:96, :] = jnp.broadcast_to(jnp.sum(v4 * v4, axis=1, keepdims=True), (32, 128))
        tmp[96:128, :] = jnp.zeros((32, 128), F32)
        ssh[c] = jnp.transpose(tmp[...])[0:1, :]
        return 0

    lax.fori_loop(0, NY, prep_h, 0)
    wait(ga[0])
    start(ga[2][0])
    wait(ga[1])
    start(ga[2][1])

    rows_h = xr[:, 0:HROWS, :].reshape(NY * HROWS, FEAT)
    pacc[...] = dot(rows_h, whi[...]) + dot(rows_h, wlo[...])

    def pack_h(c, _):
        ysh[c] = pacc[pl.ds(pl.multiple_of(c * HROWS, 32), HROWS), :].astype(BF16)
        return 0

    lax.fori_loop(0, NY, pack_h, 0)

    def scatter(i, send, ss_send, recv, ss_recv):
        copies = []
        for j, t in y_peers:
            where = at(y_=t)
            copies.append(remote(ss_send.at[t], ss_recv.at[y], y_sem.at[i, 0, j], y_sem.at[i, 1, j], where))
            copies.append(remote(send.at[t], recv.at[y], y_sem.at[i, 2, j], y_sem.at[i, 3, j], where))
        return copies

    rs_h = scatter(0, ysh, ssh, yrh, srh)
    rs_a = scatter(1, ysa, ssa, yra, sra)
    start(rs_h)

    wait(ga[2][0] + ga[2][1])
    start(ga[3][0] + ga[3][1])
    wait(ga[3][0] + ga[3][1])

    def prep_a(c, _):
        v4 = narrow_rows(ra, c)
        xr[c, 96:128, :] = v4.astype(BF16)
        tmp2[96:128, :] = jnp.broadcast_to(jnp.sum(v4 * v4, axis=1, keepdims=True), (32, 128))
        ssa[c] = jnp.transpose(tmp2[...])[0:1, :]
        return 0

    lax.fori_loop(0, NY, prep_a, 0)
    rows_a = xr[:, HROWS:128, :].reshape(NY * AROWS, FEAT)
    pacc[0:256, :] = dot(rows_a, whi[...]) + dot(rows_a, wlo[...])

    def pack_a(c, _):
        ysa[c] = pacc[pl.ds(pl.multiple_of(c * AROWS, 32), AROWS), :].astype(BF16)
        return 0

    lax.fori_loop(0, NY, pack_a, 0)
    start(rs_a)

    def transpose_x(c, _):
        lanes = pl.ds(pl.multiple_of(c * 128, 128), 128)
        xt[:, lanes] = jnp.transpose(xr[c].astype(F32)).astype(BF16)
        return 0

    lax.fori_loop(0, NY, transpose_x, 0)

    def exchange(i, zs, zss, zr, zrs):
        return [
            remote(zss, zrs, z_sem.at[i, 0], z_sem.at[i, 1], h_peer),
            remote(zs, zr, z_sem.at[i, 2], z_sem.at[i, 3], h_peer),
        ]

    zx_h = exchange(0, zsh, zssh, zrh, zrsh)
    zx_a = exchange(1, zsa, zssa, zra, zrsa)

    def sum_y(copies, n, off, send, ss_send, recv, ss_recv, zs, zss, zx):
        wait(copies)
        value = send[y].astype(F32)
        total = ss_send[y]
        for j in range(1, NY):
            t = lax.rem(y + j, NY)
            value = value + recv[t].astype(F32)
            total = total + ss_recv[t]
        zs[...] = value.astype(BF16)
        zss[...] = total
        start(zx)
        lg[off : off + n, :] = value

    sum_y(rs_h, HROWS, 0, ysh, ssh, yrh, srh, zsh, zssh, zx_h)
    sum_y(rs_a, AROWS, HROWS, ysa, ssa, yra, sra, zsa, zssa, zx_a)

    def column(row_value):
        return jnp.transpose(jnp.broadcast_to(row_value, (128, 128)))

    def row_form(col):
        return jnp.transpose(jnp.broadcast_to(col, (128, 128)))[0:1, :]

    st_z = [remote(stz.at[zl], stz.at[zl], sz_sem.at[0, j], sz_sem.at[1, j], w) for j, w in z_peers]
    st_p = [remote(stp.at[y, x], stp.at[y, x], sp_sem.at[0, i, j], sp_sem.at[1, i, j], w) for i, j, w in plane]
    st_c = [remote(stc.at[core], stc.at[core], sc_sem.at[0], sc_sem.at[1], c_peer)]

    def gather_y(buf, sem):
        return [remote(buf.at[y], buf.at[y], sem.at[0, j], sem.at[1, j], at(y_=t)) for j, t in y_peers]

    e_y, s_y = gather_y(eb, e_sem), gather_y(sc, a_sem)

    wait(zx_h)
    lg[0:HROWS, :] = lg[0:HROWS, :] + zrh[...].astype(F32)
    wait(zx_a)
    lg[HROWS:128, :] = lg[HROWS:128, :] + zra[...].astype(F32)
    scale_row = lax.rsqrt((zssh[...] + zssa[...] + zrsh[...] + zrsa[...]) / D + EPS)
    scale = column(scale_row[0:1, :])
    value = lg[...] * jnp.concatenate([scale, scale], axis=1)
    top_l = jnp.max(value, axis=1, keepdims=True)
    ex = jnp.exp(value - top_l)
    m_row = row_form(top_l)
    stc[core, 0:1, :] = m_row
    stc[core, 1:2, :] = row_form(jnp.sum(ex, axis=1, keepdims=True))
    start(st_c)
    sc[y, 0:1, :] = m_row
    sc[y, 1:2, :] = scale_row
    eb[y] = ex.astype(BF16)

    def join(parts):
        m = parts[0][0:1, :]
        for part_j in parts[1:]:
            m = jnp.maximum(m, part_j[0:1, :])
        sums = parts[0][1:2, :] * jnp.exp(parts[0][0:1, :] - m)
        for part_j in parts[1:]:
            sums = sums + part_j[1:2, :] * jnp.exp(part_j[0:1, :] - m)
        return m, sums

    wait(st_c)
    m_c, sum_c = join([stc[0], stc[1]])
    stz[zl, 0:1, :] = m_c
    stz[zl, 1:2, :] = sum_c
    start(st_z)
    start(s_y)
    start(e_y)
    wait(st_z)
    m_z, sum_z = join([stz[j] for j in range(NZL)])
    stp[y, x, 0:1, :] = m_z
    stp[y, x, 1:2, :] = sum_z
    start(st_p)

    labels = (lax.broadcasted_iota(jnp.int32, (1, COLS), 1) + rep * COLS).astype(F32)
    wait(e_y)
    wait(s_y)
    wait(st_p)

    def deltas(c, _):
        m_all, sum_all = join([stp[c, i] for i in range(NX)])
        s = column(jnp.exp(sc[c, 0:1, :] - m_all) / sum_all)
        r = column(sc[c, 1:2, :])
        t = tcol[c]
        t2 = jnp.concatenate([t, t], axis=1)
        p = eb[c].astype(F32) * jnp.concatenate([s, s], axis=1)
        delta = jnp.where(t2 >= 0.0, p - jnp.where(t2 == labels, 1.0, 0.0), 0.0)
        delta = delta * jnp.concatenate([r, r], axis=1)
        dd[pl.ds(pl.multiple_of(c * 128, 128), 128), :] = delta.astype(BF16)
        return 0

    lax.fori_loop(0, NY, deltas, 0)

    def update(b, _):
        rows = pl.ds(pl.multiple_of(b * 256, 256), 256)
        grad = dot(xt[rows, :], dd[...])
        g = gcol[rows, :] * LEARN_RATE
        w_out[rows, :] = wv[rows, :] - jnp.concatenate([g, g], axis=1) * grad
        return 0

    lax.fori_loop(0, 4, update, 0)


def on_device(queries, cache_keys, cache_values, page_table, lengths, history, norm_gain, draft_weight, targets, accepted):
    vmem = pl.BlockSpec(memory_space=pltpu.VMEM)
    smem = pltpu.SMEM
    hbm = pl.BlockSpec(memory_space=pl.ANY)
    V = pltpu.VMEM
    dma = pltpu.SemaphoreType.DMA
    attended, new_weight = pl.pallas_call(
        body,
        out_shape=(
            V((1, STEPS, FEAT), BF16),
            V((FEAT, COLS), F32),
        ),
        in_specs=[hbm] * 4 + [pl.BlockSpec(memory_space=pltpu.SMEM)] + [hbm] * 5,
        out_specs=(vmem, vmem),
        scratch_shapes=[
            smem((1, 16), jnp.int32),
            V((12, FEAT), BF16), V((1, FEAT), F32), V((16, 64), jnp.int32), V((1, 64), jnp.int32),
            V((STEPS, 2048), BF16), V((1024, HD), BF16), V((1024, HD), BF16), V((FEAT, COLS), F32),
            V((64, HD), F32), V((64, HD), F32), V((40, HD), F32), V((40, HD), F32), V((STEPS, FEAT), F32),
            V((NC, NZL, 8, FEAT), BF16), V((NC, NZL, 4, FEAT), BF16), V((NC, NZL, 4, FEAT), BF16),
            V((4, 8, FEAT), F32), V((NY, 128, FEAT), BF16), V((FEAT, 1024), BF16),
            V((FEAT, COLS), BF16), V((FEAT, COLS), BF16), V((FEAT, 128), F32), V((768, COLS), F32),
            V((128, 128), F32), V((128, 128), F32), V((16, 64), F32), V((NY, 128, 128), F32),
            V((NY, HROWS, COLS), BF16), V((NY, AROWS, COLS), BF16), V((NY, HROWS, COLS), BF16), V((NY, AROWS, COLS), BF16),
            V((NY, 1, 128), F32), V((NY, 1, 128), F32), V((NY, 1, 128), F32), V((NY, 1, 128), F32),
            V((HROWS, COLS), BF16), V((AROWS, COLS), BF16), V((HROWS, COLS), BF16), V((AROWS, COLS), BF16),
            V((1, 128), F32), V((1, 128), F32), V((1, 128), F32), V((1, 128), F32),
            V((128, COLS), F32), V((NZL, 2, 128), F32), V((NY, NX, 2, 128), F32), V((2, 2, 128), F32),
            V((NY, 128, COLS), BF16), V((NY, 2, 128), F32), V((1024, COLS), BF16),
            dma((9,)), dma((2,)), dma((3, 2, 8)), dma((3, 2, 2, 4)), dma((3, 2, 2, 4)), dma((2, 4, 8)), dma((2, 4)),
            dma((2, 8)), dma((2, 4, 8)), dma((2,)), dma((2, 8)), dma((2, 8)),
        ],
        compiler_params=pltpu.CompilerParams(collective_id=0, has_side_effects=True, vmem_limit_bytes=67043328 - 1280 * 1024),
        name="decode_draft_step",
    )(
        queries,
        cache_keys.reshape(1024, HD),
        cache_values.reshape(1024, HD),
        page_table.reshape(1, 16),
        lengths,
        history.reshape(12, FEAT),
        norm_gain.reshape(1, FEAT),
        draft_weight,
        targets.T,
        accepted.reshape(1, 64),
    )
    return attended, new_weight


def solution(mesh):
    return jax.shard_map(
        on_device,
        mesh=mesh,
        in_specs=(
            P("rep", None, None),
            P("rep", "tp", None, None, None),
            P("rep", "tp", None, None, None),
            P("rep", "tp", None),
            P("rep"),
            P("rep", None, "tp"),
            P("tp"),
            P("tp", "rep"),
            P(),
            P(),
        ),
        out_specs=(P("rep", None, "tp"), P("tp", "rep")),
        check_vma=False,
    )
```

time: 105 us -> 98.1 us (0.934)
  local copies, waits for them, and re-layouts: 6.31 us -> 1.57 us
  Pallas kernels: 97.3 us -> 95 us
    unnamed x21 -> x2, local copies, waits for them, and re-layouts: 6.31 us -> 1.57 us
    pallas_call x1, Pallas kernels: 97.3 us -> 95 us  [on_device(): pl.pallas_call(body, out_shape=(V((1, STEPS, FEAT), BF16), V((FEAT, COLS)...]
where the time goes in v2:
time: 98.1 us; the launch traced here: 97.9 us
  Pallas kernels  95 us (97%)
  local copies, waits for them, and re-layouts  1.57 us (2%)
  between operations  1.29 us (1%)
    pallas_call x1, Pallas kernels, on_device(): pl.pallas_call(body, out_shape=(V((1, STEPS, FEAT), BF16), V((FEAT, COLS)...  95 us

profile of v2, /device:TPU:1, one launch (start us, length us, event | category | flops | bytes accessed | tf_op | source)
XLA Modules:
  0.0 97.9 jit_solution(1850694127586223934)
XLA Ops:
  1.3 95.0 %decode_draft_step.1 = (bf16[1,4,1024]{2,1,0:T(4,128)(2,1)S(1)}, f32[1024,256]{1,0:T(8,128)S(1)}) custom-call(bf16[1,4,16384]{2,1,0:T(4,128)(2,1)} %q_hbm.1, bf16[1024,128]{1,0:T(8,128)(2,1)} %bitcast.7, bf16[1024,128]{1,0:T(8,128)(2,1)} %bitcast.8, s32[1,16]{1,0:T(1,128)} %bitcast.12, s32[1]{0:T(128)S(6)} %copy.16.length, bf16[12,1024]{1,0:T(8,128)(2,1)} %bitcast.9, ...), custom_call_target="tpu_custom_call" | custom-call | tf_op jit(solution)/shard_map/decode_draft_step/pallas_call | solution.py:441
  96.3 0.6 copy.14
  96.9 1.0 copy.15

commit v3 on v2

--- a/solution.py
+++ b/solution.py
@@ -50,7 +50,7 @@
     ysh, ysa, yrh, yra, ssh, ssa, srh, sra,
     zsh, zsa, zrh, zra, zssh, zssa, zrsh, zrsa,
     lg, stz, stp, stc, eb, sc, dd,
-    load_sem, px_sem, gz_sem, gx_sem, gc_sem, y_sem, z_sem, sz_sem, sp_sem, sc_sem, e_sem, a_sem,
+    load_sem, px_sem, gz_sem, gx_sem, gc_sem, y_sem, z_sem, sz_sem, sp_sem, sc_sem, e_sem,
 ):
     rep = lax.axis_index("rep")
     tp = lax.axis_index("tp")
@@ -59,7 +59,9 @@
     zl = rep // NC
     zh = lax.rem(tp, 2)
     y = tp // 2
-    cc = x * NCORE + core
+    cc = core * NX + x
+    own_base = core * NX
+    other_base = (1 - core) * NX
 
     def at(zl_=None, x_=None, core_=None, y_=None, zh_=None):
         r = ((zl if zl_ is None else zl_) * NX + (x if x_ is None else x_)) * NCORE + (core if core_ is None else core_)
@@ -78,7 +80,10 @@
         if i or j
     ]
     c_peer = at(core_=1 - core)
-    y_peers = [(j, lax.rem(y + j, NY)) for j in range(1, NY)]
+    y_half = y // 4
+    y_near = [y_half * 4 + lax.rem(lax.rem(y, 4) + j, 4) for j in range(1, 4)]
+    y_far = [(1 - y_half) * 4 + lax.rem(lax.rem(y, 4) + j, 4) for j in range(4)]
+    y_peers = list(enumerate(y_near + y_far))
     h_peer = at(zh_=1 - zh)
 
     barrier = pltpu.get_barrier_semaphore()
@@ -155,11 +160,15 @@
     px = remote(px_send, px_recv, px_sem.at[0], px_sem.at[1], h_peer)
     px.start()
 
-    def gather(buf, i):
-        z = [
-            remote(buf.at[cc, zl], buf.at[cc, zl], gz_sem.at[i, 0, j], gz_sem.at[i, 1, j], where)
-            for j, where in z_peers
-        ]
+    across = (1 - half) * 4 + lax.rem(zl, 4)
+
+    def gather(buf, i, relay):
+        def send(k, j, where):
+            return remote(buf.at[cc, k], buf.at[cc, k], gz_sem.at[i, 0, j], gz_sem.at[i, 1, j], where)
+
+        z = [send(zl, j, where) for j, where in z_peers]
+        if relay:
+            z = z[0:4] + [send(across, j + 4, where) for j, where in z_peers[0:3]]
 
         def piece(k, h):
             return buf.at[k, pl.ds(h * 4, 4)]
@@ -174,12 +183,12 @@
             )
             one = []
             for j in range(NX):
-                k = lax.rem(x + j, NX) * NCORE + core
+                k = own_base + lax.rem(x + j, NX)
                 one.append(remote(piece(k, h), piece(k, h), gc_sem.at[i, slot, 0, j], gc_sem.at[i, slot, 1, j], c_peer))
             cs.append(one)
-        return z[0:3], z[3:7], xs, cs
-
-    g8, g4, ga = gather(r8, 0), gather(r4, 1), gather(ra, 2)
+        return z[0:3], z[3:4] if relay else z[3:7], xs, cs, z[4:7]
+
+    g8, g4, ga = gather(r8, 0, True), gather(r4, 1, True), gather(ra, 2, False)
     start(g8[0] + g4[0] + g8[1] + g4[1])
 
     wait(loads[5:7])
@@ -198,6 +207,8 @@
 
     wait(g8[0] + g4[0])
     start(g8[2][0] + g4[2][0])
+    wait(g8[1] + g4[1])
+    start(g8[4] + g4[4])
 
     tmp[0:64, :] = jnp.broadcast_to(stat_rows[0:1, :], (64, 128))
     px.wait()
@@ -220,7 +231,7 @@
     start(ga[0] + ga[1])
     att_out[0] = own
 
-    wait(g8[1] + g4[1])
+    wait(g8[4] + g4[4])
     start(g8[2][1] + g4[2][1])
 
     wait(loads[7:9])
@@ -234,7 +245,7 @@
     i_of = jnp.where(rho16 < 64, 4 + lax.rem(rho16, 8), jnp.where(rho16 < 96, 12, 0) + lax.rem(rho16, 4))
 
     def target_cols(c, _):
-        pick = (rep_lane == zl_of * NC + c).astype(F32)
+        pick = (rep_lane == zl_of * NC + lax.rem(c, NX) * NCORE + c // NX).astype(F32)
         rows = lax.dot_general(
             pick, tk[...], (((1,), (1,)), ((), ())), precision=lax.Precision.HIGHEST, preferred_element_type=F32
         )
@@ -254,8 +265,6 @@
             f4[j, 0:4, :] = buf[c, 2 * j].astype(F32)
             f4[j, 4:8, :] = buf[c, 2 * j + 1].astype(F32)
         return f4[...].reshape(32, FEAT)
-
-    wait(g8[3][0] + g4[3][0] + g8[3][1] + g4[3][1])
 
     def prep_h(c, _):
         v8 = r8[c].astype(F32).reshape(64, FEAT)
@@ -268,20 +277,16 @@
         ssh[c] = jnp.transpose(tmp[...])[0:1, :]
         return 0
 
-    lax.fori_loop(0, NY, prep_h, 0)
-    wait(ga[0])
-    start(ga[2][0])
-    wait(ga[1])
-    start(ga[2][1])
-
-    rows_h = xr[:, 0:HROWS, :].reshape(NY * HROWS, FEAT)
-    pacc[...] = dot(rows_h, whi[...]) + dot(rows_h, wlo[...])
-
-    def pack_h(c, _):
-        ysh[c] = pacc[pl.ds(pl.multiple_of(c * HROWS, 32), HROWS), :].astype(BF16)
-        return 0
-
-    lax.fori_loop(0, NY, pack_h, 0)
+    def logits_h(base):
+        lax.fori_loop(0, NX, lambda k, z: prep_h(base + k, z), 0)
+        rows_h = xr[pl.ds(base, NX), 0:HROWS, :].reshape(NX * HROWS, FEAT)
+        pacc[...] = dot(rows_h, whi[...]) + dot(rows_h, wlo[...])
+
+        def pack_h(k, _):
+            ysh[base + k] = pacc[pl.ds(pl.multiple_of(k * HROWS, 32), HROWS), :].astype(BF16)
+            return 0
+
+        lax.fori_loop(0, NX, pack_h, 0)
 
     def scatter(i, send, ss_send, recv, ss_recv):
         copies = []
@@ -293,8 +298,33 @@
 
     rs_h = scatter(0, ysh, ssh, yrh, srh)
     rs_a = scatter(1, ysa, ssa, yra, sra)
-    start(rs_h)
-
+    rs_near, rs_far = rs_h[0:6], rs_h[6:14]
+    near_first = y_half == core
+    logits_h(own_base)
+
+    @pl.when(near_first)
+    def _():
+        start(rs_near)
+
+    @pl.when(jnp.logical_not(near_first))
+    def _():
+        start(rs_far)
+
+    wait(g8[3][0] + g4[3][0] + g8[3][1] + g4[3][1])
+    logits_h(other_base)
+
+    @pl.when(near_first)
+    def _():
+        start(rs_far)
+
+    @pl.when(jnp.logical_not(near_first))
+    def _():
+        start(rs_near)
+
+    wait(ga[0])
+    start(ga[2][0])
+    wait(ga[1])
+    start(ga[2][1])
     wait(ga[2][0] + ga[2][1])
     start(ga[3][0] + ga[3][1])
     wait(ga[3][0] + ga[3][1])
@@ -362,7 +392,7 @@
     def gather_y(buf, sem):
         return [remote(buf.at[y], buf.at[y], sem.at[0, j], sem.at[1, j], at(y_=t)) for j, t in y_peers]
 
-    e_y, s_y = gather_y(eb, e_sem), gather_y(sc, a_sem)
+    e_y = gather_y(eb, e_sem)
 
     wait(zx_h)
     lg[0:HROWS, :] = lg[0:HROWS, :] + zrh[...].astype(F32)
@@ -374,44 +404,45 @@
     top_l = jnp.max(value, axis=1, keepdims=True)
     ex = jnp.exp(value - top_l)
     m_row = row_form(top_l)
-    stc[core, 0:1, :] = m_row
-    stc[core, 1:2, :] = row_form(jnp.sum(ex, axis=1, keepdims=True))
+    stp[y, x, 0:1, :] = m_row
+    stp[y, x, 1:2, :] = row_form(jnp.sum(ex, axis=1, keepdims=True))
+    stp[y, x, 2:3, :] = scale_row
+    stp[y, x, 3:4, :] = jnp.zeros((1, 128), F32)
+    start(st_p)
+    eb[y] = ex.astype(BF16)
+    start(e_y)
+
+    def join(parts):
+        m = parts[0][0]
+        for part_j in parts[1:]:
+            m = jnp.maximum(m, part_j[0])
+        sums = parts[0][1] * jnp.exp(parts[0][0] - m)
+        for part_j in parts[1:]:
+            sums = sums + part_j[1] * jnp.exp(part_j[0] - m)
+        return m, sums
+
+    wait(st_p)
+    for c in range(NY):
+        m_x, sum_x = join([(stp[c, i, 0:1, :], stp[c, i, 1:2, :]) for i in range(NX)])
+        stc[core, 0, c : c + 1, :] = m_x
+        stc[core, 1, c : c + 1, :] = sum_x
+        sc[0, c : c + 1, :] = stp[c, x, 0:1, :]
     start(st_c)
-    sc[y, 0:1, :] = m_row
-    sc[y, 1:2, :] = scale_row
-    eb[y] = ex.astype(BF16)
-
-    def join(parts):
-        m = parts[0][0:1, :]
-        for part_j in parts[1:]:
-            m = jnp.maximum(m, part_j[0:1, :])
-        sums = parts[0][1:2, :] * jnp.exp(parts[0][0:1, :] - m)
-        for part_j in parts[1:]:
-            sums = sums + part_j[1:2, :] * jnp.exp(part_j[0:1, :] - m)
-        return m, sums
-
     wait(st_c)
-    m_c, sum_c = join([stc[0], stc[1]])
-    stz[zl, 0:1, :] = m_c
-    stz[zl, 1:2, :] = sum_c
+    m_c, sum_c = join([(stc[j, 0], stc[j, 1]) for j in range(NCORE)])
+    stz[zl, 0] = m_c
+    stz[zl, 1] = sum_c
     start(st_z)
-    start(s_y)
-    start(e_y)
     wait(st_z)
-    m_z, sum_z = join([stz[j] for j in range(NZL)])
-    stp[y, x, 0:1, :] = m_z
-    stp[y, x, 1:2, :] = sum_z
-    start(st_p)
+    m_all, sum_all = join([(stz[j, 0], stz[j, 1]) for j in range(NZL)])
+    sc[1] = jnp.exp(sc[0] - m_all) / sum_all
 
     labels = (lax.broadcasted_iota(jnp.int32, (1, COLS), 1) + rep * COLS).astype(F32)
     wait(e_y)
-    wait(s_y)
-    wait(st_p)
 
     def deltas(c, _):
-        m_all, sum_all = join([stp[c, i] for i in range(NX)])
-        s = column(jnp.exp(sc[c, 0:1, :] - m_all) / sum_all)
-        r = column(sc[c, 1:2, :])
+        s = column(sc[1, pl.ds(c, 1), :])
+        r = column(stp[c, 0, 2:3, :])
         t = tcol[c]
         t2 = jnp.concatenate([t, t], axis=1)
         p = eb[c].astype(F32) * jnp.concatenate([s, s], axis=1)
@@ -453,16 +484,16 @@
             V((64, HD), F32), V((64, HD), F32), V((40, HD), F32), V((40, HD), F32), V((STEPS, FEAT), F32),
             V((NC, NZL, 8, FEAT), BF16), V((NC, NZL, 4, FEAT), BF16), V((NC, NZL, 4, FEAT), BF16),
             V((4, 8, FEAT), F32), V((NY, 128, FEAT), BF16), V((FEAT, 1024), BF16),
-            V((FEAT, COLS), BF16), V((FEAT, COLS), BF16), V((FEAT, 128), F32), V((768, COLS), F32),
+            V((FEAT, COLS), BF16), V((FEAT, COLS), BF16), V((FEAT, 128), F32), V((NX * HROWS, COLS), F32),
             V((128, 128), F32), V((128, 128), F32), V((16, 64), F32), V((NY, 128, 128), F32),
             V((NY, HROWS, COLS), BF16), V((NY, AROWS, COLS), BF16), V((NY, HROWS, COLS), BF16), V((NY, AROWS, COLS), BF16),
             V((NY, 1, 128), F32), V((NY, 1, 128), F32), V((NY, 1, 128), F32), V((NY, 1, 128), F32),
             V((HROWS, COLS), BF16), V((AROWS, COLS), BF16), V((HROWS, COLS), BF16), V((AROWS, COLS), BF16),
             V((1, 128), F32), V((1, 128), F32), V((1, 128), F32), V((1, 128), F32),
-            V((128, COLS), F32), V((NZL, 2, 128), F32), V((NY, NX, 2, 128), F32), V((2, 2, 128), F32),
-            V((NY, 128, COLS), BF16), V((NY, 2, 128), F32), V((1024, COLS), BF16),
+            V((128, COLS), F32), V((NZL, 2, NY, 128), F32), V((NY, NX, 4, 128), F32), V((NCORE, 2, NY, 128), F32),
+            V((NY, 128, COLS), BF16), V((2, NY, 128), F32), V((1024, COLS), BF16),
             dma((9,)), dma((2,)), dma((3, 2, 8)), dma((3, 2, 2, 4)), dma((3, 2, 2, 4)), dma((2, 4, 8)), dma((2, 4)),
-            dma((2, 8)), dma((2, 4, 8)), dma((2,)), dma((2, 8)), dma((2, 8)),
+            dma((2, 8)), dma((2, 4, 8)), dma((2,)), dma((2, 8)),
         ],
         compiler_params=pltpu.CompilerParams(collective_id=0, has_side_effects=True, vmem_limit_bytes=67043328 - 1280 * 1024),
         name="decode_draft_step",

time: 98.1 us -> 90.6 us (0.924)
  Pallas kernels: 95 us -> 87.6 us
    pallas_call x1, Pallas kernels: 95 us -> 87.6 us  [on_device(): pl.pallas_call(body, out_shape=(V((1, STEPS, FEAT), BF16), V((FEAT, COLS)...]
where the time goes in v3:
time: 90.6 us; the launch traced here: 90.4 us
  Pallas kernels  87.6 us (97%)
  local copies, waits for them, and re-layouts  1.57 us (2%)
  between operations  1.29 us (1%)
    pallas_call x1, Pallas kernels, on_device(): pl.pallas_call(body, out_shape=(V((1, STEPS, FEAT), BF16), V((FEAT, COLS)...  87.6 us

profile of v3, /device:TPU:1, one launch (start us, length us, event | category | flops | bytes accessed | tf_op | source)
XLA Modules:
  0.0 90.4 jit_solution(12049603755734617844)
XLA Ops:
  1.3 87.6 %decode_draft_step.1 = (bf16[1,4,1024]{2,1,0:T(4,128)(2,1)S(1)}, f32[1024,256]{1,0:T(8,128)S(1)}) custom-call(bf16[1,4,16384]{2,1,0:T(4,128)(2,1)} %q_hbm.1, bf16[1024,128]{1,0:T(8,128)(2,1)} %bitcast.7, bf16[1024,128]{1,0:T(8,128)(2,1)} %bitcast.8, s32[1,16]{1,0:T(1,128)} %bitcast.12, s32[1]{0:T(128)S(6)} %copy.16.length, bf16[12,1024]{1,0:T(8,128)(2,1)} %bitcast.9, ...), custom_call_target="tpu_custom_call" | custom-call | tf_op jit(solution)/shard_map/decode_draft_step/pallas_call | solution.py:472
  88.9 0.6 copy.14
  89.5 1.0 %copy.15 = f32[1024,256]{1,0:T(8,128)} copy(f32[1024,256]{1,0:T(8,128)S(1)} %get-tuple-element.3) | data formatting | bytes 2097152
